TPU v7x, 128 devices: a whole 4x4x4 slice. The times are simulated.
128 devices in a mesh: gx: 4 (over z_lo, core), gy: 8 (over z_hi, x), gz: 4 (over y).
Axes of the slice: x: 4, y: 4, z: 4 (z_hi: 2, z_lo: 2; z = z_hi * 2 + z_lo), core: 2. Of those that a mesh axis runs over, the one named last changes fastest.
Arguments:
- velocity: float32 [6, 2097152], P(None, ('gx', 'gy', 'gz')), may hold values from -6 to 6
- positions: float32 [3, 2097152], P(None, ('gx', 'gy', 'gz')), may hold values from 0 to 100
- inverse_mass: float32 [2097152], P(('gx', 'gy', 'gz')), may hold values from 0.2 to 2
- inverse_inertia: float32 [3, 2097152], P(None, ('gx', 'gy', 'gz')), may hold values from 0.5 to 5
- normals: float32 [3, 8, 2097152], P(None, None, ('gx', 'gy', 'gz')), may hold values from -1 to 1
- lever_own: float32 [3, 8, 2097152], P(None, None, ('gx', 'gy', 'gz')), may hold values from -0.5 to 0.5
- lever_other: float32 [3, 8, 2097152], P(None, None, ('gx', 'gy', 'gz')), may hold values from -0.5 to 0.5
- speed_bias: float32 [8, 2097152], P(None, ('gx', 'gy', 'gz')), may hold values from -0.6 to 0.2
- contact_mass: float32 [8, 2097152], P(None, ('gx', 'gy', 'gz')), may hold values from 0.1 to 1
- partner_block: int32 [8, 16384], P(None, ('gx', 'gy', 'gz')), may hold values from 0 to 367
- partner_lane: int32 [8, 2097152], P(None, ('gx', 'gy', 'gz')), may hold values from 0 to 127
- slot_counts: int32 [2097152], P(('gx', 'gy', 'gz')), may hold values from 1 to 8
- ghost_blocks: int32 [6, 5120], P(None, ('gx', 'gy', 'gz')), may hold values from 0 to 127
Outputs:
- velocity_out: float32 [6, 2097152], P(None, ('gx', 'gy', 'gz'))
- positions_out: float32 [3, 2097152], P(None, ('gx', 'gy', 'gz'))
Inputs may be any that keep to these rules, and one draw needn't show every extreme that they name: `slot_counts`: slots at or beyond a body's count are padding. `ghost_blocks`: block numbers within the sending tile.
All inputs are finite; a program needn't handle non-finite values.
Results may differ from a plain program's by a relative error of at most 0.0001.
Values sent between devices are 32-bit elements; how exact they have to be, the bound alone decides.
A program may use at most 128 MiB of HBM per device.

v0:
```python
import functools

import jax
import jax.numpy as jnp
from jax import lax
from jax.experimental import pallas as pl
from jax.experimental.pallas import tpu as pltpu
from jax.sharding import PartitionSpec as P

BLOCK = 128
BLK = 128
K = 8
GHOST = 40
ITERS = 3
EXT = BLK + 6 * GHOST
FACE_ROWS = GHOST * 6
RELAXATION = 0.25
TIME_STEP = 1.0 / 60.0
MESH = pl.DeviceIdType.MESH
UNROLL = 4
FACE_OF_REGION = (1, 0, 3, 2, 5, 4)


def slot_sums(terms):
    sub = lax.broadcasted_iota(jnp.int32, (8, BLOCK), 0)

    def merge(first, second, bit):
        low = (sub & bit) == 0
        if second is None:
            return first + pltpu.roll(first, bit, 0)
        if bit == 4:
            return jnp.where(low, first, second) + pltpu.roll(jnp.where(low, second, first), 4, 0)
        up = jnp.where(low, first, second)
        other = jnp.where(low, second, first)
        return up + jnp.where(low, pltpu.roll(other, 8 - bit, 0), pltpu.roll(other, bit, 0))

    level = [merge(terms[0], terms[4], 4), merge(terms[1], terms[5], 4), merge(terms[2], None, 4), merge(terms[3], None, 4)]
    level = [merge(level[0], level[2], 2), merge(level[1], level[3], 2)]
    return merge(level[0], level[1], 1)


def kernel(
    vel_h, pos_h, im_h, ii_h, nrm_h, lo_h, lt_h, bias_h, mass_h, pb_h, lane_h, cnt_h, gb_h,
    vout, pout,
    pos, im, ii, nrm, co, ct, base, bias, mass, lane, cnt, inv, imp, vin,
    ext0, ext1, ext2, own, send, tmp, pb, gb,
    in_sem, send_sem, recv_sem,
):
    gx, gy, gz = lax.axis_index("gx"), lax.axis_index("gy"), lax.axis_index("gz")
    nx, ny, nz = lax.axis_size("gx"), lax.axis_size("gy"), lax.axis_size("gz")
    near = [
        ((gx + nx - 1) % nx, gy, gz), ((gx + 1) % nx, gy, gz),
        (gx, (gy + ny - 1) % ny, gz), (gx, (gy + 1) % ny, gz),
        (gx, gy, (gz + nz - 1) % nz), (gx, gy, (gz + 1) % nz),
    ]
    exts = [ext0, ext1, ext2]

    loads = [
        pltpu.make_async_copy(s, d, in_sem.at[i])
        for i, (s, d) in enumerate([
            (gb_h, gb), (vel_h, vin), (pb_h, pb), (nrm_h, nrm), (lo_h, co), (lt_h, ct), (bias_h, bias),
            (mass_h, mass), (cnt_h, cnt), (im_h, im), (ii_h, ii), (lane_h, lane), (pos_h, pos),
        ])
    ]
    loads[0].start()
    loads[1].start()
    barrier = pltpu.get_barrier_semaphore()
    for device in near:
        pl.semaphore_signal(barrier, inc=1, device_id=device, device_id_type=MESH)
    for load in loads[2:]:
        load.start()

    def column(b):
        return pl.ds(pl.multiple_of(b * BLOCK, BLOCK), BLOCK)

    def loop(count, body, unroll=UNROLL):
        def step(i, carry):
            for u in range(unroll):
                body(i * unroll + u, u)
            return carry
        lax.fori_loop(0, count // unroll, step, 0)

    def copies(round_number):
        made = []
        for region in range(6):
            face = FACE_OF_REGION[region]
            made.append(pltpu.make_async_remote_copy(
                src_ref=send.at[round_number, pl.ds(face * FACE_ROWS, FACE_ROWS)],
                dst_ref=exts[round_number].at[pl.ds((BLK + region * GHOST) * 6, FACE_ROWS)],
                send_sem=send_sem.at[round_number, face],
                recv_sem=recv_sem.at[round_number, face],
                device_id=near[face],
                device_id_type=MESH,
            ))
        return made

    def pack_faces(round_number):
        def body(g, u):
            for face in range(6):
                send[round_number, pl.ds(face * FACE_ROWS + g * 6, 6), :] = own[pl.ds(gb[face, g] * 8, 6), :]
        loop(GHOST, body, 4)

    loads[1].wait()

    def unpack(b, u):
        rows = vin[:, column(b)]
        own[pl.ds(pl.multiple_of(b * 8, 8), 6), :] = rows
        ext0[pl.ds(b * 6, 6), :] = rows
    loop(BLK, unpack)
    loads[0].wait()
    pack_faces(0)
    pl.semaphore_wait(barrier, 6)
    pending = copies(0)
    for copy in pending:
        copy.start()

    for load in loads[2:]:
        load.wait()

    slot_index = lax.broadcasted_iota(jnp.int32, (K, BLOCK), 0)

    def base_of(b, n, c_own, own_rows):
        total = bias[:, column(b)]
        for c in range(3):
            total = total - n[c] * own_rows(c)
            total = total - c_own[c] * own_rows(c + 3)
        base[:, column(b)] = total

    def cross(first, second):
        return [
            first[1] * second[2] - first[2] * second[1],
            first[2] * second[0] - first[0] * second[2],
            first[0] * second[1] - first[1] * second[0],
        ]

    def prepare(b, u):
        cols = column(b)
        n = [nrm[c, :, cols] for c in range(3)]
        c_own = cross([co[c, :, cols] for c in range(3)], n)
        c_other = cross([ct[c, :, cols] for c in range(3)], n)
        for c in range(3):
            co[c, :, cols] = c_own[c]
            ct[c, :, cols] = c_other[c]
        live = slot_index < jnp.broadcast_to(cnt[pl.ds(b, 1), :], (K, BLOCK))
        mass[:, cols] = jnp.where(live, RELAXATION * mass[:, cols], 0.0)
        row = pl.multiple_of(b * 8, 8)
        inv[pl.ds(row, 3), :] = jnp.broadcast_to(im[pl.ds(b, 1), :], (3, BLOCK))
        inv[pl.ds(row + 3, 3), :] = ii[:, cols]
        base_of(b, n, c_own, lambda c: jnp.broadcast_to(own[pl.ds(row + c, 1), :], (K, BLOCK)))
    loop(BLK, prepare, 2)

    for it in range(ITERS):
        ext = exts[it]
        for copy in pending:
            copy.wait()
        last = it == ITERS - 1

        def sweep(b, u):
            cols = column(b)
            stage = u * 64
            for k in range(K):
                tmp[pl.ds(stage + 8 * k, 8), :] = ext[pl.ds(pb[k, b] * 6, 8), :]
            lanes = lane[:, cols]
            n = [nrm[c, :, cols] for c in range(3)]
            c_own = [co[c, :, cols] for c in range(3)]
            total = base[:, cols]
            for c in range(6):
                rows = tmp[pl.ds(stage + c, 8, stride=8), :]
                picked = jnp.take_along_axis(rows, lanes, axis=1, mode="promise_in_bounds")
                total = total + (n[c] if c < 3 else ct[c - 3, :, cols]) * picked
            step = mass[:, cols] * total
            if it == 0:
                change = jnp.maximum(-step, 0.0)
                new = change
            else:
                old = imp[:, cols]
                new = jnp.maximum(old - step, 0.0)
                change = new - old
            if not last:
                imp[:, cols] = new
            sums = slot_sums([change * (n[c] if c < 3 else c_own[c - 3]) for c in range(6)])
            row = pl.multiple_of(b * 8, 8)
            moved = (own[pl.ds(row, 8), :] - inv[pl.ds(row, 8), :] * sums)[:6]
            if last:
                vout[:, cols] = moved
                pout[:, cols] = pos[:, cols] + TIME_STEP * moved[:3]
            else:
                own[pl.ds(row, 6), :] = moved
                exts[it + 1][pl.ds(b * 6, 6), :] = moved
        loop(BLK, sweep)

        if not last:
            pack_faces(it + 1)
            pending = copies(it + 1)
            for copy in pending:
                copy.start()

            def rebase(b, u):
                cols = column(b)
                row = pl.multiple_of(b * 8, 8)
                base_of(
                    b, [nrm[c, :, cols] for c in range(3)], [co[c, :, cols] for c in range(3)],
                    lambda c: jnp.broadcast_to(own[pl.ds(row + c, 1), :], (K, BLOCK)),
                )
            loop(BLK, rebase)


def per_device(
    velocity, positions, inverse_mass, inverse_inertia, normals, lever_own, lever_other, speed_bias, contact_mass,
    partner_block, partner_lane, slot_counts, ghost_blocks,
):
    bodies = BLK * BLOCK
    slots = pltpu.VMEM((K, bodies), jnp.float32)
    vectors = pltpu.VMEM((3, K, bodies), jnp.float32)
    table = pltpu.VMEM((EXT * 6 + 8, BLOCK), jnp.float32)
    hbm = pl.BlockSpec(memory_space=pl.ANY)
    vmem = pl.BlockSpec(memory_space=pltpu.VMEM)
    return pl.pallas_call(
        kernel,
        out_shape=(
            jax.ShapeDtypeStruct((6, bodies), jnp.float32),
            jax.ShapeDtypeStruct((3, bodies), jnp.float32),
        ),
        in_specs=[hbm] * 13,
        out_specs=(vmem, vmem),
        scratch_shapes=[
            pltpu.VMEM((3, bodies), jnp.float32),
            pltpu.VMEM((BLK, BLOCK), jnp.float32),
            pltpu.VMEM((3, bodies), jnp.float32),
            vectors, vectors, vectors,
            slots, slots, slots,
            pltpu.VMEM((K, bodies), jnp.int32),
            pltpu.VMEM((BLK, BLOCK), jnp.int32),
            pltpu.VMEM((BLK * 8, BLOCK), jnp.float32),
            slots,
            pltpu.VMEM((6, bodies), jnp.float32),
            table, table, table,
            pltpu.VMEM((BLK * 8, BLOCK), jnp.float32),
            pltpu.VMEM((ITERS, 6 * FACE_ROWS, BLOCK), jnp.float32),
            pltpu.VMEM((UNROLL * 64, BLOCK), jnp.float32),
            pltpu.SMEM((K, BLK), jnp.int32),
            pltpu.SMEM((6, GHOST), jnp.int32),
            pltpu.SemaphoreType.DMA((13,)),
            pltpu.SemaphoreType.DMA((ITERS, 6)),
            pltpu.SemaphoreType.DMA((ITERS, 6)),
        ],
        compiler_params=pltpu.CompilerParams(collective_id=0, has_side_effects=True),
    )(
        velocity, positions, inverse_mass.reshape(BLK, BLOCK), inverse_inertia, normals, lever_own, lever_other,
        speed_bias, contact_mass, partner_block, partner_lane, slot_counts.reshape(BLK, BLOCK), ghost_blocks,
    )


def solution(mesh):
    every = ("gx", "gy", "gz")
    flat, wide, deep = P(every), P(None, every), P(None, None, every)
    return jax.shard_map(
        per_device,
        mesh=mesh,
        in_specs=(wide, wide, flat, wide, deep, deep, deep, wide, wide, wide, wide, flat, wide),
        out_specs=(wide, wide),
        check_vma=False,
    )
```

profile of v0, /device:TPU:1, one launch (start us, length us, event | category | flops | bytes accessed | tf_op | source)
XLA Modules:
  0.0 52.2 jit_solution(17190463988826054473)
XLA Ops:
  0.6 48.0 %shard_map.140 = (f32[6,16384]{1,0:T(8,128)}, f32[3,16384]{1,0:T(4,128)}) custom-call(f32[6,16384]{1,0:T(8,128)} %vel_h.1, f32[3,16384]{1,0:T(4,128)} %pos_h.1, f32[128,128]{1,0:T(8,128)} %bitcast.2, f32[3,16384]{1,0:T(4,128)} %ii_h.1, f32[3,8,16384]{2,1,0:T(8,128)} %nrm_h.1, f32[3,8,16384]{2,1,0:T(8,128)} %lo_h.1, f32[3,8,16384]{2,1,0:T(8,128)} %lt_h.1, ...), custom_call_target="tpu_custom_call" | custom-call | tf_op jit(solution)/shard_map/pallas_call | solution.py:218
  48.6 1.9 %copy.17 = f32[6,16384]{1,0:T(8,128)} copy(f32[6,16384]{1,0:T(8,128)} %get-tuple-element.4) | data formatting | bytes 786432
  50.5 1.7 %copy.18 = f32[3,16384]{1,0:T(4,128)} copy(f32[3,16384]{1,0:T(4,128)} %get-tuple-element.5) | data formatting | bytes 393216
where the time goes:
time: 52.4 us; the launch traced here: 52.2 us
  Pallas kernels  48 us (92%)
  local copies, waits for them, and re-layouts  3.57 us (7%)
  between operations  0.64 us (1%)
    pallas_call x1, Pallas kernels, per_device(): pl.pallas_call(kernel, out_shape=(jax.ShapeDtypeStruct((6, bodies), jnp.f...  48 us
    unnamed x2, local copies, waits for them, and re-layouts  3.57 us

commit v1 on v0

--- a/solution.py
+++ b/solution.py
@@ -18,6 +18,7 @@
 TIME_STEP = 1.0 / 60.0
 MESH = pl.DeviceIdType.MESH
 UNROLL = 4
+GROUP = 16
 FACE_OF_REGION = (1, 0, 3, 2, 5, 4)
 
 
@@ -25,25 +26,20 @@
     sub = lax.broadcasted_iota(jnp.int32, (8, BLOCK), 0)
 
     def merge(first, second, bit):
-        low = (sub & bit) == 0
         if second is None:
             return first + pltpu.roll(first, bit, 0)
-        if bit == 4:
-            return jnp.where(low, first, second) + pltpu.roll(jnp.where(low, second, first), 4, 0)
-        up = jnp.where(low, first, second)
-        other = jnp.where(low, second, first)
-        return up + jnp.where(low, pltpu.roll(other, 8 - bit, 0), pltpu.roll(other, bit, 0))
-
-    level = [merge(terms[0], terms[4], 4), merge(terms[1], terms[5], 4), merge(terms[2], None, 4), merge(terms[3], None, 4)]
-    level = [merge(level[0], level[2], 2), merge(level[1], level[3], 2)]
-    return merge(level[0], level[1], 1)
+        low = (sub & bit) == 0
+        return jnp.where(low, first, second) + pltpu.roll(jnp.where(low, second, first), bit, 0)
+
+    pairs = [merge(terms[0], terms[1], 1), merge(terms[2], terms[3], 1), merge(terms[4], terms[5], 1)]
+    return merge(merge(pairs[0], pairs[1], 2), merge(pairs[2], None, 2), 4)
 
 
 def kernel(
     vel_h, pos_h, im_h, ii_h, nrm_h, lo_h, lt_h, bias_h, mass_h, pb_h, lane_h, cnt_h, gb_h,
     vout, pout,
     pos, im, ii, nrm, co, ct, base, bias, mass, lane, cnt, inv, imp, vin,
-    ext0, ext1, ext2, own, send, tmp, pb, gb,
+    ext0, ext1, ext2, own, send, tmp, got, pb, gb, rows_of,
     in_sem, send_sem, recv_sem,
 ):
     gx, gy, gz = lax.axis_index("gx"), lax.axis_index("gy"), lax.axis_index("gz")
@@ -142,52 +138,91 @@
             co[c, :, cols] = c_own[c]
             ct[c, :, cols] = c_other[c]
         live = slot_index < jnp.broadcast_to(cnt[pl.ds(b, 1), :], (K, BLOCK))
-        mass[:, cols] = jnp.where(live, RELAXATION * mass[:, cols], 0.0)
+        mass[:, cols] = jnp.where(live, -RELAXATION * mass[:, cols], 0.0)
         row = pl.multiple_of(b * 8, 8)
         inv[pl.ds(row, 3), :] = jnp.broadcast_to(im[pl.ds(b, 1), :], (3, BLOCK))
         inv[pl.ds(row + 3, 3), :] = ii[:, cols]
         base_of(b, n, c_own, lambda c: jnp.broadcast_to(own[pl.ds(row + c, 1), :], (K, BLOCK)))
     loop(BLK, prepare, 2)
 
+    def place(b, u):
+        for k in range(K):
+            rows_of[b * K + k] = pb[k, b] * 6
+    loop(BLK, place, 2)
+
     for it in range(ITERS):
         ext = exts[it]
         for copy in pending:
             copy.wait()
         last = it == ITERS - 1
 
-        def sweep(b, u):
-            cols = column(b)
-            stage = u * 64
-            for k in range(K):
-                tmp[pl.ds(stage + 8 * k, 8), :] = ext[pl.ds(pb[k, b] * 6, 8), :]
-            lanes = lane[:, cols]
-            n = [nrm[c, :, cols] for c in range(3)]
-            c_own = [co[c, :, cols] for c in range(3)]
-            total = base[:, cols]
-            for c in range(6):
-                rows = tmp[pl.ds(stage + c, 8, stride=8), :]
-                picked = jnp.take_along_axis(rows, lanes, axis=1, mode="promise_in_bounds")
-                total = total + (n[c] if c < 3 else ct[c - 3, :, cols]) * picked
-            step = mass[:, cols] * total
-            if it == 0:
-                change = jnp.maximum(-step, 0.0)
-                new = change
+        def gather(i):
+            rows = rows_of.at[pl.ds(i * (GROUP * K), GROUP * K)]
+            for j in range(GROUP * K):
+                tmp[pl.ds(j * 9, 8), :] = ext[pl.ds(rows[j], 8), :]
+
+        def span(i):
+            return pl.ds(pl.multiple_of(i * (GROUP * BLOCK), GROUP * BLOCK), GROUP * BLOCK)
+
+        def part(u):
+            return pl.ds(u * BLOCK, BLOCK)
+
+        def permute(i):
+            lane_g = lane.at[:, span(i)]
+            for u in range(GROUP):
+                lanes = lane_g[:, part(u)]
+                for c in range(6):
+                    rows = tmp[pl.ds(u * 72 + c, 8, stride=9), :]
+                    got[pl.ds((u * 6 + c) * 8, 8), :] = jnp.take_along_axis(rows, lanes, axis=1, mode="promise_in_bounds")
+
+        def update(i):
+            wide = span(i)
+            base_g, mass_g, imp_g = (r.at[:, wide] for r in (base, mass, imp))
+            n_g, own_cross, other_cross = ([r.at[c, :, wide] for c in range(3)] for r in (nrm, co, ct))
+            row = pl.multiple_of(i * (GROUP * 8), GROUP * 8)
+            own_g, inv_g = own.at[pl.ds(row, GROUP * 8)], inv.at[pl.ds(row, GROUP * 8)]
+            if last:
+                vout_g, pout_g, pos_g = (r.at[:, wide] for r in (vout, pout, pos))
             else:
-                old = imp[:, cols]
-                new = jnp.maximum(old - step, 0.0)
-                change = new - old
-            if not last:
-                imp[:, cols] = new
-            sums = slot_sums([change * (n[c] if c < 3 else c_own[c - 3]) for c in range(6)])
-            row = pl.multiple_of(b * 8, 8)
-            moved = (own[pl.ds(row, 8), :] - inv[pl.ds(row, 8), :] * sums)[:6]
-            if last:
-                vout[:, cols] = moved
-                pout[:, cols] = pos[:, cols] + TIME_STEP * moved[:3]
-            else:
-                own[pl.ds(row, 6), :] = moved
-                exts[it + 1][pl.ds(b * 6, 6), :] = moved
-        loop(BLK, sweep)
+                ext_g = exts[it + 1].at[pl.ds(pl.multiple_of(i * (GROUP * 6), GROUP * 6), GROUP * 6)]
+            for u in range(GROUP):
+                cols = part(u)
+                n = [n_g[c][:, cols] for c in range(3)]
+                terms = [
+                    (n[c] if c < 3 else other_cross[c - 3][:, cols]) * got[pl.ds((u * 6 + c) * 8, 8), :]
+                    for c in range(6)
+                ]
+                total = ((terms[0] + terms[1]) + (terms[2] + terms[3])) + ((terms[4] + terms[5]) + base_g[:, cols])
+                step = mass_g[:, cols] * total
+                if it == 0:
+                    change = jnp.maximum(step, 0.0)
+                    new = change
+                else:
+                    old = imp_g[:, cols]
+                    new = jnp.maximum(old + step, 0.0)
+                    change = new - old
+                if not last:
+                    imp_g[:, cols] = new
+                sums = slot_sums([change * (n[c] if c < 3 else own_cross[c - 3][:, cols]) for c in range(6)])
+                moved = (own_g[pl.ds(u * 8, 8), :] - inv_g[pl.ds(u * 8, 8), :] * sums)[:6]
+                if last:
+                    vout_g[:, cols] = moved
+                    pout_g[:, cols] = pos_g[:, cols] + TIME_STEP * moved[:3]
+                else:
+                    own_g[pl.ds(u * 8, 6), :] = moved
+                    ext_g[pl.ds(u * 6, 6), :] = moved
+
+        groups = BLK // GROUP
+        gather(0)
+        permute(0)
+        gather(1)
+
+        def stages(i, carry):
+            update(i)
+            permute(jnp.minimum(i + 1, groups - 1))
+            gather(jnp.minimum(i + 2, groups - 1))
+            return carry
+        lax.fori_loop(0, groups, stages, 0)
 
         if not last:
             pack_faces(it + 1)
@@ -237,9 +272,11 @@
             table, table, table,
             pltpu.VMEM((BLK * 8, BLOCK), jnp.float32),
             pltpu.VMEM((ITERS, 6 * FACE_ROWS, BLOCK), jnp.float32),
-            pltpu.VMEM((UNROLL * 64, BLOCK), jnp.float32),
+            pltpu.VMEM((GROUP * 72 + 16, BLOCK), jnp.float32),
+            pltpu.VMEM((GROUP * 48, BLOCK), jnp.float32),
             pltpu.SMEM((K, BLK), jnp.int32),
             pltpu.SMEM((6, GHOST), jnp.int32),
+            pltpu.SMEM((BLK * K,), jnp.int32),
             pltpu.SemaphoreType.DMA((13,)),
             pltpu.SemaphoreType.DMA((ITERS, 6)),
             pltpu.SemaphoreType.DMA((ITERS, 6)),

time: 52.4 us -> 41.3 us (0.79)
  Pallas kernels: 48 us -> 36.9 us
    pallas_call x1, Pallas kernels: 48 us -> 36.9 us  [per_device(): pl.pallas_call(kernel, out_shape=(jax.ShapeDtypeStruct((6, bodies), jnp.f...]
where the time goes in v1:
time: 41.3 us; the launch traced here: 41.1 us
  Pallas kernels  36.9 us (89%)
  local copies, waits for them, and re-layouts  3.57 us (9%)
  between operations  0.64 us (2%)
    pallas_call x1, Pallas kernels, per_device(): pl.pallas_call(kernel, out_shape=(jax.ShapeDtypeStruct((6, bodies), jnp.f...  36.9 us
    unnamed x2, local copies, waits for them, and re-layouts  3.57 us

profile of v1, /device:TPU:1, one launch (start us, length us, event | category | flops | bytes accessed | tf_op | source)
XLA Modules:
  0.0 41.1 jit_solution(94917374614603904)
XLA Ops:
  0.6 36.9 %shard_map.140 = (f32[6,16384]{1,0:T(8,128)}, f32[3,16384]{1,0:T(4,128)}) custom-call(f32[6,16384]{1,0:T(8,128)} %vel_h.1, f32[3,16384]{1,0:T(4,128)} %pos_h.1, f32[128,128]{1,0:T(8,128)} %bitcast.2, f32[3,16384]{1,0:T(4,128)} %ii_h.1, f32[3,8,16384]{2,1,0:T(8,128)} %nrm_h.1, f32[3,8,16384]{2,1,0:T(8,128)} %lo_h.1, f32[3,8,16384]{2,1,0:T(8,128)} %lt_h.1, ...), custom_call_target="tpu_custom_call" | custom-call | tf_op jit(solution)/shard_map/pallas_call | solution.py:253
  37.5 1.9 %copy.17 = f32[6,16384]{1,0:T(8,128)} copy(f32[6,16384]{1,0:T(8,128)} %get-tuple-element.4) | data formatting | bytes 786432
  39.4 1.7 %copy.18 = f32[3,16384]{1,0:T(4,128)} copy(f32[3,16384]{1,0:T(4,128)} %get-tuple-element.5) | data formatting | bytes 393216

commit v2 on v1

--- a/solution.py
+++ b/solution.py
@@ -240,6 +240,14 @@
             loop(BLK, rebase)
 
 
+def finish(moved, placed, vel_out, pos_out, sems):
+    writes = [pltpu.make_async_copy(moved, vel_out, sems.at[0]), pltpu.make_async_copy(placed, pos_out, sems.at[1])]
+    for write in writes:
+        write.start()
+    for write in writes:
+        write.wait()
+
+
 def per_device(
     velocity, positions, inverse_mass, inverse_inertia, normals, lever_own, lever_other, speed_bias, contact_mass,
     partner_block, partner_lane, slot_counts, ghost_blocks,
@@ -250,12 +258,9 @@
     table = pltpu.VMEM((EXT * 6 + 8, BLOCK), jnp.float32)
     hbm = pl.BlockSpec(memory_space=pl.ANY)
     vmem = pl.BlockSpec(memory_space=pltpu.VMEM)
-    return pl.pallas_call(
+    moved, placed = pl.pallas_call(
         kernel,
-        out_shape=(
-            jax.ShapeDtypeStruct((6, bodies), jnp.float32),
-            jax.ShapeDtypeStruct((3, bodies), jnp.float32),
-        ),
+        out_shape=(pltpu.VMEM((6, bodies), jnp.float32), pltpu.VMEM((3, bodies), jnp.float32)),
         in_specs=[hbm] * 13,
         out_specs=(vmem, vmem),
         scratch_shapes=[
@@ -286,6 +291,16 @@
         velocity, positions, inverse_mass.reshape(BLK, BLOCK), inverse_inertia, normals, lever_own, lever_other,
         speed_bias, contact_mass, partner_block, partner_lane, slot_counts.reshape(BLK, BLOCK), ghost_blocks,
     )
+    return pl.pallas_call(
+        finish,
+        out_shape=(
+            jax.ShapeDtypeStruct((6, bodies), jnp.float32),
+            jax.ShapeDtypeStruct((3, bodies), jnp.float32),
+        ),
+        in_specs=[vmem, vmem],
+        out_specs=(hbm, hbm),
+        scratch_shapes=[pltpu.SemaphoreType.DMA((2,))],
+    )(pltpu.with_memory_space_constraint(moved, pltpu.VMEM), pltpu.with_memory_space_constraint(placed, pltpu.VMEM))
 
 
 def solution(mesh):

time: 41.3 us -> 37.8 us (0.915)
  local copies, waits for them, and re-layouts: 3.57 us -> 0 us
    unnamed x2 -> x0, local copies, waits for them, and re-layouts: 3.57 us -> none
    pallas_call x1 -> x2, Pallas kernels: 36.9 us -> 37.1 us  [the longest x1 36.2 us: per_device(): pl.pallas_call(kernel, out_shape=(pltpu.VMEM((6, bodies), jnp.float32), p...]
where the time goes in v2:
time: 37.8 us; the launch traced here: 37.7 us
  Pallas kernels  37.1 us (98%)
  between operations  0.64 us (2%)
    pallas_call x1, Pallas kernels, per_device(): pl.pallas_call(kernel, out_shape=(pltpu.VMEM((6, bodies), jnp.float32), p...  36.2 us
    pallas_call x1, Pallas kernels, per_device(): pl.pallas_call(finish, out_shape=(jax.ShapeDtypeStruct((6, bodies), jnp.f...  0.89 us

profile of v2, /device:TPU:1, one launch (start us, length us, event | category | flops | bytes accessed | tf_op | source)
XLA Modules:
  0.0 37.7 jit_solution(2347079734328501041)
XLA Ops:
  0.6 36.2 %shard_map.140 = (f32[6,16384]{1,0:T(8,128)S(1)}, f32[3,16384]{1,0:T(4,128)S(1)}) custom-call(f32[6,16384]{1,0:T(8,128)} %vel_h.1, f32[3,16384]{1,0:T(4,128)} %pos_h.1, f32[128,128]{1,0:T(8,128)} %bitcast.2, f32[3,16384]{1,0:T(4,128)} %ii_h.1, f32[3,8,16384]{2,1,0:T(8,128)} %nrm_h.1, f32[3,8,16384]{2,1,0:T(8,128)} %lo_h.1, f32[3,8,16384]{2,1,0:T(8,128)} %lt_h.1, ...), custom_call_target="tpu_custom_call" | custom-call | tf_op jit(solution)/shard_map/pallas_call | solution.py:261
  36.8 0.9 %shard_map.141 = (f32[6,16384]{1,0:T(8,128)}, f32[3,16384]{1,0:T(4,128)}) custom-call(f32[6,16384]{1,0:T(8,128)S(1)} %get-tuple-element.4.moved, f32[3,16384]{1,0:T(4,128)S(1)} %get-tuple-element.5.placed), custom_call_target="tpu_custom_call" | custom-call | tf_op jit(solution)/shard_map/pallas_call | solution.py:294

commit v3 on v2

v3 whole, which is shorter than its diff:
```python
import functools

import jax
import jax.numpy as jnp
from jax import lax
from jax.experimental import pallas as pl
from jax.experimental.pallas import tpu as pltpu
from jax.sharding import PartitionSpec as P

BLOCK = 128
BLK = 128
K = 8
GHOST = 40
ITERS = 3
EXT = BLK + 6 * GHOST
FACE_ROWS = GHOST * 6
RELAXATION = 0.25
TIME_STEP = 1.0 / 60.0
MESH = pl.DeviceIdType.MESH
UNROLL = 4
GROUP = 16
SEND_ROW, BLOCK_AT, PLACE_OF = 8, 16, 24
NORMAL, OWN_CROSS, OTHER_CROSS, BASE, BIAS, MASS, IMPULSE, PLANES = 0, 3, 6, 9, 10, 11, 12, 13
ROW = 4


def slot_sums(terms):
    sub = lax.broadcasted_iota(jnp.int32, (8, BLOCK), 0)

    def merge(first, second, bit):
        if second is None:
            return first + pltpu.roll(first, bit, 0)
        low = (sub & bit) == 0
        return jnp.where(low, first, second) + pltpu.roll(jnp.where(low, second, first), bit, 0)

    pairs = [merge(terms[0], terms[1], 1), merge(terms[2], terms[3], 1), merge(terms[4], terms[5], 1)]
    return merge(merge(pairs[0], pairs[1], 2), merge(pairs[2], None, 2), 4)


def pick_lanes(rows, lanes):
    numbers = lax.GatherDimensionNumbers(
        offset_dims=(), collapsed_slice_dims=(1,), start_index_map=(1,),
        operand_batching_dims=(0,), start_indices_batching_dims=(0,),
    )
    return lax.gather(rows, lanes[:, :, None], numbers, (1, 1), mode=lax.GatherScatterMode.PROMISE_IN_BOUNDS)


def kernel(
    vel_h, pos_h, im_h, ii_h, nrm_h, lo_h, lt_h, bias_h, mass_h, pb_h, lane_h, cnt_h, gb_h,
    vout, pout,
    pos, im, ii, raw, slots, raw_lane, lane, cnt, bodies, vin,
    ext0, ext1, ext2, send, tmp, got, pb, gb, entries, ranks, tables, block_of, send_rows, place_row, rows_of,
    in_sem, send_sem, recv_sem,
):
    gx, gy, gz = lax.axis_index("gx"), lax.axis_index("gy"), lax.axis_index("gz")
    nx, ny, nz = lax.axis_size("gx"), lax.axis_size("gy"), lax.axis_size("gz")
    near = [
        ((gx + nx - 1) % nx, gy, gz), ((gx + 1) % nx, gy, gz),
        (gx, (gy + ny - 1) % ny, gz), (gx, (gy + 1) % ny, gz),
        (gx, gy, (gz + nz - 1) % nz), (gx, gy, (gz + 1) % nz),
    ]
    exts = [ext0, ext1, ext2]
    own, inv = bodies.at[0], bodies.at[1]
    nrm, co, ct = (slots.at[pl.ds(first, 3)] for first in (NORMAL, OWN_CROSS, OTHER_CROSS))
    base, bias, mass = (slots.at[which] for which in (BASE, BIAS, MASS))

    loads = [
        pltpu.make_async_copy(s, d, in_sem.at[i])
        for i, (s, d) in enumerate([
            (gb_h, gb), (vel_h, vin), (pb_h, pb), (nrm_h, raw.at[pl.ds(0, 3)]), (lo_h, raw.at[pl.ds(3, 3)]), (lt_h, raw.at[pl.ds(6, 3)]), (bias_h, raw.at[9]),
            (mass_h, raw.at[10]), (cnt_h, cnt), (im_h, im), (ii_h, ii), (lane_h, raw_lane), (pos_h, pos),
        ])
    ]
    for load in loads[:3]:
        load.start()
    barrier = pltpu.get_barrier_semaphore()
    for device in near:
        pl.semaphore_signal(barrier, inc=1, device_id=device, device_id_type=MESH)
    for load in loads[3:]:
        load.start()

    def column(b):
        return pl.ds(pl.multiple_of(b * BLOCK, BLOCK), BLOCK)

    def loop(count, body, unroll=UNROLL):
        def step(i, carry):
            for u in range(unroll):
                body(i * unroll + u, u)
            return carry
        lax.fori_loop(0, count // unroll, step, 0)

    far_x = gx % 2
    far_y = jnp.where(gy % ROW == 0, 2, 3)
    far_x_near = (jnp.where(far_x == 0, near[0][0], near[1][0]), gy, gz)
    pair_near = (jnp.where(far_x == 0, near[1][0], near[0][0]), gy, gz)
    far_y_near = (gx, jnp.where(far_y == 2, near[2][1], near[3][1]), gz)
    short_y_near = (gx, jnp.where(far_y == 2, near[3][1], near[2][1]), gz)
    first_face = [(far_x, far_x_near)]
    second_face = [(far_y, far_y_near)]
    other_faces = [(4, near[4]), (5, near[5]), (5 - far_y, short_y_near), (1 - far_x, pair_near)]

    def face_copy(round_number, face, device):
        region = face + 1 - 2 * (face % 2)
        return pltpu.make_async_remote_copy(
            src_ref=send.at[round_number, pl.ds(face * FACE_ROWS, FACE_ROWS)],
            dst_ref=exts[round_number].at[pl.ds((BLK + region * GHOST) * 6, FACE_ROWS)],
            send_sem=send_sem.at[round_number, face],
            recv_sem=recv_sem.at[round_number, face],
            device_id=device,
            device_id_type=MESH,
        )

    def receive(round_number):
        for face in range(6):
            face_copy(round_number, face, near[face]).wait()

    def send_faces(round_number, faces):
        def body(g, u):
            for face, _ in faces:
                row = send_rows[face * GHOST + g]
                send[round_number, pl.ds(face * FACE_ROWS + g * 6, 6), :] = own[pl.ds(row, 6), :]
        loop(GHOST, body, 4)
        for face, device in faces:
            face_copy(round_number, face, device).start()

    loads[0].wait()
    loads[2].wait()
    down = lax.broadcasted_iota(jnp.int32, (BLK, BLK), 0)
    across = lax.broadcasted_iota(jnp.int32, (BLK, BLK), 1)
    sublane = lax.broadcasted_iota(jnp.int32, (8, BLK), 0)
    number = lax.broadcasted_iota(jnp.int32, (8, BLK), 1)
    found = jnp.zeros((8, BLK), jnp.int32)
    for face in range(6):
        row = jnp.zeros((8, BLK), jnp.int32)
        for g in range(GHOST):
            row = jnp.where(number == g, gb[face, g], row)
        found = jnp.where(sublane == face, row, found)
    entries[...] = found

    def in_face(face):
        found = jnp.broadcast_to(entries[pl.ds(face, 1), :], (BLK, BLK)) == down
        return jnp.sum(jnp.where(found & (across < GHOST), 1, 0), axis=1, keepdims=True) > 0

    def to_row(column):
        return jnp.sum(jnp.where(down == across, column, 0), axis=0, keepdims=True)

    def to_column(row):
        return jnp.sum(jnp.where(down == across, row, 0), axis=1, keepdims=True)

    key = jnp.where(in_face(far_x), 0, jnp.where(in_face(far_y), BLK, 2 * BLK)) + down[:, :1]
    place_of = jnp.sum(jnp.where(key < to_row(key), 1, 0), axis=0, keepdims=True)
    block_at = jnp.sum(jnp.where(to_column(place_of) == across, down, 0), axis=0, keepdims=True)
    place_of, block_at = (jnp.broadcast_to(jnp.clip(row, 0, BLK - 1), (8, BLK)) for row in (place_of, block_at))
    partner = pick_lanes(pb[...], block_at)
    partner_place = pick_lanes(place_of, jnp.minimum(partner, BLK - 1))
    ranks[pl.ds(0, 8), :] = 6 * jnp.where(partner < BLK, partner_place, partner)
    ranks[pl.ds(SEND_ROW, 8), :] = 8 * pick_lanes(place_of, entries[...])
    ranks[pl.ds(BLOCK_AT, 8), :] = block_at
    ranks[pl.ds(PLACE_OF, 8), :] = place_of
    to_scalars = pltpu.make_async_copy(ranks, tables, in_sem.at[0])
    to_scalars.start()
    to_scalars.wait()

    def bounded(value, most):
        return jnp.minimum(jnp.maximum(value, 0), most)

    def orders(b, u):
        block_of[b] = bounded(tables[BLOCK_AT, b], BLK - 1)
    loop(BLK, orders)

    def entry_rows(g, u):
        for face in range(6):
            send_rows[face * GHOST + g] = bounded(tables[SEND_ROW + face, g], (BLK - 1) * 8)
    loop(GHOST, entry_rows)

    loads[1].wait()

    def unpack(i, u):
        rows = vin[:, pl.ds(block_of[i] * BLOCK, BLOCK)]
        own[pl.ds(pl.multiple_of(i * 8, 8), 6), :] = rows
        ext0[pl.ds(i * 6, 6), :] = rows
    loop(BLK, unpack)

    pl.semaphore_wait(barrier, 6)
    for faces in (first_face, second_face, other_faces):
        send_faces(0, faces)

    for load in loads[3:]:
        load.wait()

    slot_index = lax.broadcasted_iota(jnp.int32, (K, BLOCK), 0)

    def base_of(b, n, c_own, own_rows, total):
        for c in range(3):
            total = total - n[c] * own_rows(c)
            total = total - c_own[c] * own_rows(c + 3)
        base[:, column(b)] = total

    def cross(first, second):
        return [
            first[1] * second[2] - first[2] * second[1],
            first[2] * second[0] - first[0] * second[2],
            first[0] * second[1] - first[1] * second[0],
        ]

    def prepare(i, u):
        b = block_of[i]
        cols = column(i)
        source = [raw[c, :, pl.ds(b * BLOCK, BLOCK)] for c in range(11)]
        n = source[:3]
        c_own = cross([source[3 + c] for c in range(3)], n)
        c_other = cross([source[6 + c] for c in range(3)], n)
        target = slots.at[:, :, cols]
        for c in range(3):
            target[NORMAL + c] = n[c]
            target[OWN_CROSS + c] = c_own[c]
            target[OTHER_CROSS + c] = c_other[c]
        lane[:, cols] = raw_lane[:, pl.ds(b * BLOCK, BLOCK)]
        live = slot_index < jnp.broadcast_to(cnt[pl.ds(b, 1), :], (K, BLOCK))
        target[MASS] = jnp.where(live, -RELAXATION * source[10], 0.0)
        target[BIAS] = source[9]
        row = pl.multiple_of(i * 8, 8)
        inv[pl.ds(row, 3), :] = jnp.broadcast_to(im[pl.ds(b, 1), :], (3, BLOCK))
        inv[pl.ds(row + 3, 3), :] = ii[:, pl.ds(b * BLOCK, BLOCK)]
        base_of(i, n, c_own, lambda c: jnp.broadcast_to(own[pl.ds(row + c, 1), :], (K, BLOCK)), source[9])
    loop(BLK, prepare, 2)

    def scalars(i, u):
        place_row[i] = bounded(tables[PLACE_OF, i], BLK - 1) * 8
        for k in range(K):
            rows_of[i * K + k] = bounded(tables[k, i], (EXT - 1) * 6)
    loop(BLK, scalars, 2)

    for it in range(ITERS):
        ext = exts[it]
        receive(it)
        last = it == ITERS - 1

        def gather(rows_at):
            for u, rows in enumerate(rows_at):
                for k in range(K):
                    tmp[pl.ds((u * K + k) * 9, 8), :] = ext[pl.ds(rows[k], 8), :]

        def permute(lanes_of):
            for u, lanes in enumerate(lanes_of):
                for c in range(6):
                    rows = tmp[pl.ds(u * 72 + c, 8, stride=9), :]
                    got[pl.ds((u * 6 + c) * 8, 8), :] = pick_lanes(rows, lanes)

        def impulse_and_moved(u, plane, own_b, inv_b):
            normal = [plane(NORMAL + c) for c in range(3)]
            terms = [(normal[c] if c < 3 else plane(OTHER_CROSS + c - 3)) * got[pl.ds((u * 6 + c) * 8, 8), :] for c in range(6)]
            total = ((terms[0] + terms[1]) + (terms[2] + terms[3])) + ((terms[4] + terms[5]) + plane(BASE))
            step = plane(MASS) * total
            if it == 0:
                new = jnp.maximum(step, 0.0)
                change = new
            else:
                old = plane(IMPULSE)
                new = jnp.maximum(old + step, 0.0)
                change = new - old
            sums = slot_sums([change * (normal[c] if c < 3 else plane(OWN_CROSS + c - 3)) for c in range(6)])
            return new, (own_b - inv_b * sums)[:6]

        def wide(i):
            return pl.ds(pl.multiple_of(i * (GROUP * BLOCK), GROUP * BLOCK), GROUP * BLOCK)

        def rows_at(i):
            rows = rows_of.at[pl.ds(i * (GROUP * K), GROUP * K)]
            return [[rows[u * K + k] for k in range(K)] for u in range(GROUP)]

        def lanes_at(i):
            lane_g = lane.at[:, wide(i)]
            return [lane_g[:, pl.ds(u * BLOCK, BLOCK)] for u in range(GROUP)]

        def update(i):
            slots_g = slots.at[:, :, wide(i)]
            bodies_g = bodies.at[:, pl.ds(pl.multiple_of(i * (GROUP * 8), GROUP * 8), GROUP * 8)]
            if not last:
                ext_g = exts[it + 1].at[pl.ds(pl.multiple_of(i * (GROUP * 6), GROUP * 6), GROUP * 6)]
            for u in range(GROUP):
                cols, row = pl.ds(u * BLOCK, BLOCK), pl.ds(u * 8, 8)
                new, moved = impulse_and_moved(u, lambda p: slots_g[p, :, cols], bodies_g[0, row, :], bodies_g[1, row, :])
                bodies_g[0, pl.ds(u * 8, 6), :] = moved
                if not last:
                    slots_g[IMPULSE, :, cols] = new
                    ext_g[pl.ds(u * 6, 6), :] = moved

        groups = BLK // GROUP

        def stages(i, carry):
            update(i)
            permute(lanes_at(jnp.minimum(i + 1, groups - 1)))
            gather(rows_at(jnp.minimum(i + 2, groups - 1)))
            return carry

        gather(rows_at(0))
        permute(lanes_at(0))
        gather(rows_at(1))
        if last:
            lax.fori_loop(0, groups, stages, 0)

            def finished(b, u):
                cols = column(b)
                moved = own[pl.ds(place_row[b], 6), :]
                vout[:, cols] = moved
                pout[:, cols] = pos[:, cols] + TIME_STEP * moved[:3]
            loop(BLK, finished)
        else:
            done = 0
            for blocks, faces in ((GHOST, first_face), (2 * GHOST, second_face), (BLK, other_faces)):
                until = -(-blocks // GROUP)
                lax.fori_loop(done, until, stages, 0)
                send_faces(it + 1, faces)
                done = until

            def rebase(b, u):
                cols = column(b)
                row = pl.multiple_of(b * 8, 8)
                base_of(
                    b, [nrm[c, :, cols] for c in range(3)], [co[c, :, cols] for c in range(3)],
                    lambda c: jnp.broadcast_to(own[pl.ds(row + c, 1), :], (K, BLOCK)), bias[:, cols],
                )
            loop(BLK, rebase)


def finish(moved, placed, vel_out, pos_out, sems):
    writes = [pltpu.make_async_copy(moved, vel_out, sems.at[0]), pltpu.make_async_copy(placed, pos_out, sems.at[1])]
    for write in writes:
        write.start()
    for write in writes:
        write.wait()


def per_device(
    velocity, positions, inverse_mass, inverse_inertia, normals, lever_own, lever_other, speed_bias, contact_mass,
    partner_block, partner_lane, slot_counts, ghost_blocks,
):
    bodies = BLK * BLOCK
    table = pltpu.VMEM((EXT * 6 + 8, BLOCK), jnp.float32)
    hbm = pl.BlockSpec(memory_space=pl.ANY)
    vmem = pl.BlockSpec(memory_space=pltpu.VMEM)
    moved, placed = pl.pallas_call(
        kernel,
        out_shape=(pltpu.VMEM((6, bodies), jnp.float32), pltpu.VMEM((3, bodies), jnp.float32)),
        in_specs=[hbm] * 13,
        out_specs=(vmem, vmem),
        scratch_shapes=[
            pltpu.VMEM((3, bodies), jnp.float32),
            pltpu.VMEM((BLK, BLOCK), jnp.float32),
            pltpu.VMEM((3, bodies), jnp.float32),
            pltpu.VMEM((11, K, bodies), jnp.float32),
            pltpu.VMEM((PLANES, K, bodies), jnp.float32),
            pltpu.VMEM((K, bodies), jnp.int32),
            pltpu.VMEM((K, bodies), jnp.int32),
            pltpu.VMEM((BLK, BLOCK), jnp.int32),
            pltpu.VMEM((2, BLK * 8, BLOCK), jnp.float32),
            pltpu.VMEM((6, bodies), jnp.float32),
            table, table, table,
            pltpu.VMEM((ITERS, 6 * FACE_ROWS, BLOCK), jnp.float32),
            pltpu.VMEM((GROUP * 72 + 16, BLOCK), jnp.float32),
            pltpu.VMEM((GROUP * 48, BLOCK), jnp.float32),
            pltpu.VMEM((K, BLK), jnp.int32),
            pltpu.SMEM((6, GHOST), jnp.int32),
            pltpu.VMEM((8, BLK), jnp.int32),
            pltpu.VMEM((32, BLK), jnp.int32),
            pltpu.SMEM((32, BLK), jnp.int32),
            pltpu.SMEM((BLK,), jnp.int32),
            pltpu.SMEM((6 * GHOST,), jnp.int32),
            pltpu.SMEM((BLK,), jnp.int32),
            pltpu.SMEM((BLK * K,), jnp.int32),
            pltpu.SemaphoreType.DMA((13,)),
            pltpu.SemaphoreType.DMA((ITERS, 6)),
            pltpu.SemaphoreType.DMA((ITERS, 6)),
        ],
        compiler_params=pltpu.CompilerParams(collective_id=0, has_side_effects=True),
    )(
        velocity, positions, inverse_mass.reshape(BLK, BLOCK), inverse_inertia, normals, lever_own, lever_other,
        speed_bias, contact_mass, partner_block, partner_lane, slot_counts.reshape(BLK, BLOCK), ghost_blocks,
    )
    return pl.pallas_call(
        finish,
        out_shape=(
            jax.ShapeDtypeStruct((6, bodies), jnp.float32),
            jax.ShapeDtypeStruct((3, bodies), jnp.float32),
        ),
        in_specs=[vmem, vmem],
        out_specs=(hbm, hbm),
        scratch_shapes=[pltpu.SemaphoreType.DMA((2,))],
    )(pltpu.with_memory_space_constraint(moved, pltpu.VMEM), pltpu.with_memory_space_constraint(placed, pltpu.VMEM))


def solution(mesh):
    every = ("gx", "gy", "gz")
    flat, wide, deep = P(every), P(None, every), P(None, None, every)
    return jax.shard_map(
        per_device,
        mesh=mesh,
        in_specs=(wide, wide, flat, wide, deep, deep, deep, wide, wide, wide, wide, flat, wide),
        out_specs=(wide, wide),
        check_vma=False,
    )
```

time: 37.8 us -> 36.3 us (0.960)
  Pallas kernels: 37.1 us -> 35.4 us
    pallas_call x1, Pallas kernels: 36.2 us -> 34.5 us  [per_device(): pl.pallas_call(kernel, out_shape=(pltpu.VMEM((6, bodies), jnp.float32), p...]
where the time goes in v3:
time: 36.3 us; the launch traced here: 36 us
  Pallas kernels  35.4 us (98%)
  between operations  0.64 us (2%)
    pallas_call x1, Pallas kernels, per_device(): pl.pallas_call(kernel, out_shape=(pltpu.VMEM((6, bodies), jnp.float32), p...  34.5 us
    pallas_call x1, Pallas kernels, per_device(): pl.pallas_call(finish, out_shape=(jax.ShapeDtypeStruct((6, bodies), jnp.f...  0.89 us

profile of v3, /device:TPU:1, one launch (start us, length us, event | category | flops | bytes accessed | tf_op | source)
XLA Modules:
  0.0 36.0 jit_solution(16950448081833444027)
XLA Ops:
  0.6 34.5 %shard_map.140 = (f32[6,16384]{1,0:T(8,128)S(1)}, f32[3,16384]{1,0:T(4,128)S(1)}) custom-call(f32[6,16384]{1,0:T(8,128)} %vel_h.1, f32[3,16384]{1,0:T(4,128)} %pos_h.1, f32[128,128]{1,0:T(8,128)} %bitcast.2, f32[3,16384]{1,0:T(4,128)} %ii_h.1, f32[3,8,16384]{2,1,0:T(8,128)} %nrm_h.1, f32[3,8,16384]{2,1,0:T(8,128)} %lo_h.1, f32[3,8,16384]{2,1,0:T(8,128)} %lt_h.1, ...), custom_call_target="tpu_custom_call" | custom-call | tf_op jit(solution)/shard_map/pallas_call | solution.py:343
  35.1 0.9 %shard_map.141 = (f32[6,16384]{1,0:T(8,128)}, f32[3,16384]{1,0:T(4,128)}) custom-call(f32[6,16384]{1,0:T(8,128)S(1)} %get-tuple-element.4.moved, f32[3,16384]{1,0:T(4,128)S(1)} %get-tuple-element.5.placed), custom_call_target="tpu_custom_call" | custom-call | tf_op jit(solution)/shard_map/pallas_call | solution.py:381

commit v4 on v3

--- a/solution.py
+++ b/solution.py
@@ -14,6 +14,7 @@
 ITERS = 3
 EXT = BLK + 6 * GHOST
 FACE_ROWS = GHOST * 6
+TABLE_ROWS = 4096
 RELAXATION = 0.25
 TIME_STEP = 1.0 / 60.0
 MESH = pl.DeviceIdType.MESH
@@ -114,16 +115,28 @@
         for face in range(6):
             face_copy(round_number, face, near[face]).wait()
 
+    def start_faces(round_number, faces):
+        for face, device in faces:
+            face_copy(round_number, face, device).start()
+
     def send_faces(round_number, faces):
         def body(g, u):
             for face, _ in faces:
                 row = send_rows[face * GHOST + g]
                 send[round_number, pl.ds(face * FACE_ROWS + g * 6, 6), :] = own[pl.ds(row, 6), :]
         loop(GHOST, body, 4)
-        for face, device in faces:
-            face_copy(round_number, face, device).start()
+        start_faces(round_number, faces)
 
     loads[0].wait()
+    loads[1].wait()
+
+    def pack(g, u):
+        for face in range(6):
+            send[0, pl.ds(face * FACE_ROWS + g * 6, 6), :] = vin[:, pl.ds(gb[face, g] * BLOCK, BLOCK)]
+    loop(GHOST, pack)
+    pl.semaphore_wait(barrier, 6)
+    start_faces(0, first_face + second_face + other_faces)
+
     loads[2].wait()
     down = lax.broadcasted_iota(jnp.int32, (BLK, BLK), 0)
     across = lax.broadcasted_iota(jnp.int32, (BLK, BLK), 1)
@@ -154,26 +167,22 @@
     partner = pick_lanes(pb[...], block_at)
     partner_place = pick_lanes(place_of, jnp.minimum(partner, BLK - 1))
     ranks[pl.ds(0, 8), :] = 6 * jnp.where(partner < BLK, partner_place, partner)
-    ranks[pl.ds(SEND_ROW, 8), :] = 8 * pick_lanes(place_of, entries[...])
+    ranks[pl.ds(SEND_ROW, 8), :] = pick_lanes(place_of, entries[...])
     ranks[pl.ds(BLOCK_AT, 8), :] = block_at
     ranks[pl.ds(PLACE_OF, 8), :] = place_of
     to_scalars = pltpu.make_async_copy(ranks, tables, in_sem.at[0])
     to_scalars.start()
     to_scalars.wait()
 
-    def bounded(value, most):
-        return jnp.minimum(jnp.maximum(value, 0), most)
-
     def orders(b, u):
-        block_of[b] = bounded(tables[BLOCK_AT, b], BLK - 1)
+        block_of[b] = tables[BLOCK_AT, b] & (BLK - 1)
     loop(BLK, orders)
 
     def entry_rows(g, u):
         for face in range(6):
-            send_rows[face * GHOST + g] = bounded(tables[SEND_ROW + face, g], (BLK - 1) * 8)
+            send_rows[face * GHOST + g] = (tables[SEND_ROW + face, g] & (BLK - 1)) * 8
     loop(GHOST, entry_rows)
 
-    loads[1].wait()
 
     def unpack(i, u):
         rows = vin[:, pl.ds(block_of[i] * BLOCK, BLOCK)]
@@ -181,9 +190,6 @@
         ext0[pl.ds(i * 6, 6), :] = rows
     loop(BLK, unpack)
 
-    pl.semaphore_wait(barrier, 6)
-    for faces in (first_face, second_face, other_faces):
-        send_faces(0, faces)
 
     for load in loads[3:]:
         load.wait()
@@ -226,9 +232,9 @@
     loop(BLK, prepare, 2)
 
     def scalars(i, u):
-        place_row[i] = bounded(tables[PLACE_OF, i], BLK - 1) * 8
+        place_row[i] = (tables[PLACE_OF, i] & (BLK - 1)) * 8
         for k in range(K):
-            rows_of[i * K + k] = bounded(tables[k, i], (EXT - 1) * 6)
+            rows_of[i * K + k] = tables[k, i] & (TABLE_ROWS - 1)
     loop(BLK, scalars, 2)
 
     for it in range(ITERS):
@@ -337,7 +343,7 @@
     partner_block, partner_lane, slot_counts, ghost_blocks,
 ):
     bodies = BLK * BLOCK
-    table = pltpu.VMEM((EXT * 6 + 8, BLOCK), jnp.float32)
+    table = pltpu.VMEM((TABLE_ROWS + 8, BLOCK), jnp.float32)
     hbm = pl.BlockSpec(memory_space=pl.ANY)
     vmem = pl.BlockSpec(memory_space=pltpu.VMEM)
     moved, placed = pl.pallas_call(

time: 36.3 us -> 35.5 us (0.978)
  Pallas kernels: 35.4 us -> 34.7 us
    pallas_call x1, Pallas kernels: 34.5 us -> 33.8 us  [per_device(): pl.pallas_call(kernel, out_shape=(pltpu.VMEM((6, bodies), jnp.float32), p...]
where the time goes in v4:
time: 35.5 us; the launch traced here: 35.4 us
  Pallas kernels  34.7 us (98%)
  between operations  0.64 us (2%)
    pallas_call x1, Pallas kernels, per_device(): pl.pallas_call(kernel, out_shape=(pltpu.VMEM((6, bodies), jnp.float32), p...  33.8 us
    pallas_call x1, Pallas kernels, per_device(): pl.pallas_call(finish, out_shape=(jax.ShapeDtypeStruct((6, bodies), jnp.f...  0.89 us

profile of v4, /device:TPU:1, one launch (start us, length us, event | category | flops | bytes accessed | tf_op | source)
XLA Modules:
  0.0 35.4 jit_solution(15660286685101787459)
XLA Ops:
  0.6 33.8 %shard_map.140 = (f32[6,16384]{1,0:T(8,128)S(1)}, f32[3,16384]{1,0:T(4,128)S(1)}) custom-call(f32[6,16384]{1,0:T(8,128)} %vel_h.1, f32[3,16384]{1,0:T(4,128)} %pos_h.1, f32[128,128]{1,0:T(8,128)} %bitcast.2, f32[3,16384]{1,0:T(4,128)} %ii_h.1, f32[3,8,16384]{2,1,0:T(8,128)} %nrm_h.1, f32[3,8,16384]{2,1,0:T(8,128)} %lo_h.1, f32[3,8,16384]{2,1,0:T(8,128)} %lt_h.1, ...), custom_call_target="tpu_custom_call" | custom-call | tf_op jit(solution)/shard_map/pallas_call | solution.py:349
  34.5 0.9 %shard_map.141 = (f32[6,16384]{1,0:T(8,128)}, f32[3,16384]{1,0:T(4,128)}) custom-call(f32[6,16384]{1,0:T(8,128)S(1)} %get-tuple-element.4.moved, f32[3,16384]{1,0:T(4,128)S(1)} %get-tuple-element.5.placed), custom_call_target="tpu_custom_call" | custom-call | tf_op jit(solution)/shard_map/pallas_call | solution.py:387

commit v5 on v4

--- a/solution.py
+++ b/solution.py
@@ -124,7 +124,7 @@
             for face, _ in faces:
                 row = send_rows[face * GHOST + g]
                 send[round_number, pl.ds(face * FACE_ROWS + g * 6, 6), :] = own[pl.ds(row, 6), :]
-        loop(GHOST, body, 4)
+        loop(GHOST, body, 20)
         start_faces(round_number, faces)
 
     loads[0].wait()
@@ -311,7 +311,7 @@
                 moved = own[pl.ds(place_row[b], 6), :]
                 vout[:, cols] = moved
                 pout[:, cols] = pos[:, cols] + TIME_STEP * moved[:3]
-            loop(BLK, finished)
+            loop(BLK, finished, 32)
         else:
             done = 0
             for blocks, faces in ((GHOST, first_face), (2 * GHOST, second_face), (BLK, other_faces)):

time: 35.5 us -> 35.1 us (0.989)
  Pallas kernels: 34.7 us -> 34.3 us
    pallas_call x1, Pallas kernels: 33.8 us -> 33.5 us  [per_device(): pl.pallas_call(kernel, out_shape=(pltpu.VMEM((6, bodies), jnp.float32), p...]
where the time goes in v5:
time: 35.1 us; the launch traced here: 35 us
  Pallas kernels  34.3 us (98%)
  between operations  0.64 us (2%)
    pallas_call x1, Pallas kernels, per_device(): pl.pallas_call(kernel, out_shape=(pltpu.VMEM((6, bodies), jnp.float32), p...  33.5 us
    pallas_call x1, Pallas kernels, per_device(): pl.pallas_call(finish, out_shape=(jax.ShapeDtypeStruct((6, bodies), jnp.f...  0.89 us

profile of v5, /device:TPU:1, one launch (start us, length us, event | category | flops | bytes accessed | tf_op | source)
XLA Modules:
  0.0 35.0 jit_solution(7931815712585651670)
XLA Ops:
  0.6 33.5 %shard_map.140 = (f32[6,16384]{1,0:T(8,128)S(1)}, f32[3,16384]{1,0:T(4,128)S(1)}) custom-call(f32[6,16384]{1,0:T(8,128)} %vel_h.1, f32[3,16384]{1,0:T(4,128)} %pos_h.1, f32[128,128]{1,0:T(8,128)} %bitcast.2, f32[3,16384]{1,0:T(4,128)} %ii_h.1, f32[3,8,16384]{2,1,0:T(8,128)} %nrm_h.1, f32[3,8,16384]{2,1,0:T(8,128)} %lo_h.1, f32[3,8,16384]{2,1,0:T(8,128)} %lt_h.1, ...), custom_call_target="tpu_custom_call" | custom-call | tf_op jit(solution)/shard_map/pallas_call | solution.py:349
  34.1 0.9 %shard_map.141 = (f32[6,16384]{1,0:T(8,128)}, f32[3,16384]{1,0:T(4,128)}) custom-call(f32[6,16384]{1,0:T(8,128)S(1)} %get-tuple-element.4.moved, f32[3,16384]{1,0:T(4,128)S(1)} %get-tuple-element.5.placed), custom_call_target="tpu_custom_call" | custom-call | tf_op jit(solution)/shard_map/pallas_call | solution.py:387

commit v6 on v5

--- a/solution.py
+++ b/solution.py
@@ -20,6 +20,7 @@
 MESH = pl.DeviceIdType.MESH
 UNROLL = 4
 GROUP = 16
+LAST_GROUP = 32
 SEND_ROW, BLOCK_AT, PLACE_OF = 8, 16, 24
 NORMAL, OWN_CROSS, OTHER_CROSS, BASE, BIAS, MASS, IMPULSE, PLANES = 0, 3, 6, 9, 10, 11, 12, 13
 ROW = 4
@@ -241,6 +242,7 @@
         ext = exts[it]
         receive(it)
         last = it == ITERS - 1
+        size = LAST_GROUP if last else GROUP
 
         def gather(rows_at):
             for u, rows in enumerate(rows_at):
@@ -269,22 +271,22 @@
             return new, (own_b - inv_b * sums)[:6]
 
         def wide(i):
-            return pl.ds(pl.multiple_of(i * (GROUP * BLOCK), GROUP * BLOCK), GROUP * BLOCK)
+            return pl.ds(pl.multiple_of(i * (size * BLOCK), size * BLOCK), size * BLOCK)
 
         def rows_at(i):
-            rows = rows_of.at[pl.ds(i * (GROUP * K), GROUP * K)]
-            return [[rows[u * K + k] for k in range(K)] for u in range(GROUP)]
+            rows = rows_of.at[pl.ds(i * (size * K), size * K)]
+            return [[rows[u * K + k] for k in range(K)] for u in range(size)]
 
         def lanes_at(i):
             lane_g = lane.at[:, wide(i)]
-            return [lane_g[:, pl.ds(u * BLOCK, BLOCK)] for u in range(GROUP)]
+            return [lane_g[:, pl.ds(u * BLOCK, BLOCK)] for u in range(size)]
 
         def update(i):
             slots_g = slots.at[:, :, wide(i)]
-            bodies_g = bodies.at[:, pl.ds(pl.multiple_of(i * (GROUP * 8), GROUP * 8), GROUP * 8)]
+            bodies_g = bodies.at[:, pl.ds(pl.multiple_of(i * (size * 8), size * 8), size * 8)]
             if not last:
-                ext_g = exts[it + 1].at[pl.ds(pl.multiple_of(i * (GROUP * 6), GROUP * 6), GROUP * 6)]
-            for u in range(GROUP):
+                ext_g = exts[it + 1].at[pl.ds(pl.multiple_of(i * (size * 6), size * 6), size * 6)]
+            for u in range(size):
                 cols, row = pl.ds(u * BLOCK, BLOCK), pl.ds(u * 8, 8)
                 new, moved = impulse_and_moved(u, lambda p: slots_g[p, :, cols], bodies_g[0, row, :], bodies_g[1, row, :])
                 bodies_g[0, pl.ds(u * 8, 6), :] = moved
@@ -292,7 +294,7 @@
                     slots_g[IMPULSE, :, cols] = new
                     ext_g[pl.ds(u * 6, 6), :] = moved
 
-        groups = BLK // GROUP
+        groups = BLK // size
 
         def stages(i, carry):
             update(i)
@@ -315,7 +317,7 @@
         else:
             done = 0
             for blocks, faces in ((GHOST, first_face), (2 * GHOST, second_face), (BLK, other_faces)):
-                until = -(-blocks // GROUP)
+                until = -(-blocks // size)
                 lax.fori_loop(done, until, stages, 0)
                 send_faces(it + 1, faces)
                 done = until
@@ -364,8 +366,8 @@
             pltpu.VMEM((6, bodies), jnp.float32),
             table, table, table,
             pltpu.VMEM((ITERS, 6 * FACE_ROWS, BLOCK), jnp.float32),
-            pltpu.VMEM((GROUP * 72 + 16, BLOCK), jnp.float32),
-            pltpu.VMEM((GROUP * 48, BLOCK), jnp.float32),
+            pltpu.VMEM((LAST_GROUP * 72 + 16, BLOCK), jnp.float32),
+            pltpu.VMEM((LAST_GROUP * 48, BLOCK), jnp.float32),
             pltpu.VMEM((K, BLK), jnp.int32),
             pltpu.SMEM((6, GHOST), jnp.int32),
             pltpu.VMEM((8, BLK), jnp.int32),

time: 35.1 us -> 35.1 us (level)
  no operation moved by 1% of the time
where the time goes in v6:
time: 35.1 us; the launch traced here: 35 us
  Pallas kernels  34.3 us (98%)
  between operations  0.64 us (2%)
    pallas_call x1, Pallas kernels, per_device(): pl.pallas_call(kernel, out_shape=(pltpu.VMEM((6, bodies), jnp.float32), p...  33.5 us
    pallas_call x1, Pallas kernels, per_device(): pl.pallas_call(finish, out_shape=(jax.ShapeDtypeStruct((6, bodies), jnp.f...  0.89 us

profile of v6, /device:TPU:1, one launch (start us, length us, event | category | flops | bytes accessed | tf_op | source)
XLA Modules:
  0.0 35.0 jit_solution(11105861205252335998)
XLA Ops:
  0.6 33.5 %shard_map.140 = (f32[6,16384]{1,0:T(8,128)S(1)}, f32[3,16384]{1,0:T(4,128)S(1)}) custom-call(f32[6,16384]{1,0:T(8,128)} %vel_h.1, f32[3,16384]{1,0:T(4,128)} %pos_h.1, f32[128,128]{1,0:T(8,128)} %bitcast.2, f32[3,16384]{1,0:T(4,128)} %ii_h.1, f32[3,8,16384]{2,1,0:T(8,128)} %nrm_h.1, f32[3,8,16384]{2,1,0:T(8,128)} %lo_h.1, f32[3,8,16384]{2,1,0:T(8,128)} %lt_h.1, ...), custom_call_target="tpu_custom_call" | custom-call | tf_op jit(solution)/shard_map/pallas_call | solution.py:351
  34.1 0.9 %shard_map.141 = (f32[6,16384]{1,0:T(8,128)}, f32[3,16384]{1,0:T(4,128)}) custom-call(f32[6,16384]{1,0:T(8,128)S(1)} %get-tuple-element.4.moved, f32[3,16384]{1,0:T(4,128)S(1)} %get-tuple-element.5.placed), custom_call_target="tpu_custom_call" | custom-call | tf_op jit(solution)/shard_map/pallas_call | solution.py:389
